TPU v7x, 256 devices: a whole 4x4x8 slice. The times are simulated.
256 devices in a mesh: node: 4 (over x), replica: 64 (over z, y, core).
Axes of the slice: x: 4, y: 4, z: 8, core: 2. Of those that a mesh axis runs over, the one named last changes fastest.
Arguments:
- inputs: bfloat16 [131072, 1024], P(('node', 'replica')), may hold values from -8 to 8
- grads_out: bfloat16 [131072, 1024], P(('node', 'replica')), may hold values from -1 to 1
- lengths: int32 [1024], P(('node', 'replica')), may hold values from 32 to 128
- w_in: bfloat16 [1024, 2048], P(None, 'node'), may hold values from -0.5 to 0.5
- bias_in: bfloat16 [2048], P('node'), may hold values from -3 to 3
- w_out: bfloat16 [2048, 1024], P('node'), may hold values from -0.4 to 0.4
Outputs:
- grad_w_in: float32 [1024, 2048], P('replica', 'node')
- grad_w_out: float32 [2048, 1024], P(('node', 'replica'))
- grad_bias_in: float32 [2048], P(('node', 'replica'))
- grad_bias_out: float32 [1024], P(('node', 'replica'))
All inputs are finite; a program needn't handle non-finite values.
Results may differ from a plain program's by a relative error of at most 0.0003.
Values may be sent and summed in bfloat16 or wider, within the bound.
A program may use at most 64 MiB of HBM per device.

v0:
```python
import jax
import jax.numpy as jnp
from jax import lax
from jax.sharding import PartitionSpec as P

SEQ = 128


root_half = 0.7071067811865476
inv_root_tau = 0.3989422804014327
eps_norm = 1e-06


def copy_for_each(array, axis):
    peers = lax.axis_size(axis)
    return lax.all_to_all(
        jnp.broadcast_to(array[None], (peers, *array.shape)), axis, 0, 0, tiled=True
    )


def over_copies(array, axis):
    everything = copy_for_each(array, axis)
    return jnp.sum(everything, axis=0)


def from_partner(value, axis, apart):
    mask = 2**apart
    pairs = [(source, source ^ mask) for source in range(lax.axis_size(axis))]
    return lax.ppermute(value, axis, pairs)


def in_one_piece(arrays, axis, dim, along):
    both = jnp.concatenate(arrays, axis=along)
    filled, at, outs = (lax.all_gather(both, axis, axis=dim, tiled=True), 0, [])
    for a in arrays:
        outs.append(lax.slice_in_dim(filled, at, at + a.shape[along], axis=along))
        at += a.shape[along]
    return tuple(outs)


def masked_cotangent(grads_out, lengths):
    row_count = grads_out.shape[0]
    position = lax.broadcasted_iota(jnp.int32, (row_count // SEQ, SEQ), 1)
    keep_mask = (position < lengths[:, None]).reshape(row_count, 1)
    return jnp.where(keep_mask, grads_out, jnp.zeros_like(grads_out))


def layer_grads(inputs, cotangent, w_in, bias_in, w_out):
    preact = jnp.dot(inputs, w_in, preferred_element_type=jnp.float32) + bias_in.astype(jnp.float32)
    normal_cdf = 0.5 * (1.0 + jax.scipy.special.erf(preact * root_half))
    activated = (preact * normal_cdf).astype(jnp.bfloat16)
    grad_act = lax.dot_general(
        cotangent, w_out, (((1,), (1,)), ((), ())), preferred_element_type=jnp.float32
    )
    grad_pre = grad_act * (normal_cdf + preact * inv_root_tau * jnp.exp(-0.5 * preact * preact))
    grad_half = grad_pre.astype(jnp.bfloat16)
    grad_in = lax.dot_general(
        inputs, grad_half, (((0,), (0,)), ((), ())), preferred_element_type=jnp.float32
    )
    grad_out = lax.dot_general(
        activated, cotangent, (((0,), (0,)), ((), ())), preferred_element_type=jnp.float32
    )
    return (grad_in, grad_out, jnp.sum(grad_pre, 0), jnp.sum(cotangent.astype(jnp.float32), 0))


def weigh_pair(first_parts, second_parts, totals):
    merged = []
    for index_now in range(len(first_parts)):
        cross = totals[index_now][0]
        first_sq = totals[index_now][1]
        second_sq = totals[index_now][2]
        first_coef = 1.0 - cross / (2.0 * (first_sq + eps_norm))
        second_coef = 1.0 - cross / (2.0 * (second_sq + eps_norm))
        merged.append(first_coef * first_parts[index_now] + second_coef * second_parts[index_now])
    return merged


def group_totals(partial_value, bit_pos, depth_count):
    summed = over_copies(partial_value, "node")
    for other_bit in range(bit_pos, depth_count):
        summed = summed + from_partner(summed, "replica", other_bit)
    return summed


def body(inputs, grads_out, lengths, w_in, bias_in, w_out):
    cotangent = masked_cotangent(grads_out, lengths)
    node_count = lax.axis_size("node")
    width_model = inputs.shape[1]
    pieces = in_one_piece((inputs, cotangent), "node", 0, 1)
    terms = layer_grads(pieces[0], pieces[1], w_in, bias_in, w_out)
    sums = tuple((term_now for term_now in terms))
    share = width_model // node_count
    bias_share = lax.dynamic_slice_in_dim(sums[3], lax.axis_index("node") * share, share)
    grad_parts = [sums[0], sums[1], sums[2], bias_share]
    depth_count = lax.axis_size("replica").bit_length() - 1
    replica_index = lax.axis_index("replica")
    for level_now in range(depth_count):
        bit_pos = depth_count - 1 - level_now
        is_lower = replica_index >> bit_pos & 1 == 0
        kept_parts = []
        sent_parts = []
        for part_now in grad_parts:
            middle = part_now.shape[0] // 2
            first_half = part_now[:middle]
            second_half = part_now[middle:]
            kept_parts.append(jnp.where(is_lower, first_half, second_half))
            sent_parts.append(jnp.where(is_lower, second_half, first_half))
        packed = jnp.concatenate([sent_now.reshape(-1) for sent_now in sent_parts])
        returned = from_partner(packed, "replica", bit_pos)
        first_parts = []
        second_parts = []
        offset = 0
        for kept_now in kept_parts:
            count_now = kept_now.size
            other_now = returned[offset : offset + count_now].reshape(kept_now.shape)
            offset = offset + count_now
            first_parts.append(jnp.where(is_lower, kept_now, other_now))
            second_parts.append(jnp.where(is_lower, other_now, kept_now))
        partial_value = jnp.stack(
            [
                jnp.stack(
                    [
                        jnp.sum(first_part * second_part),
                        jnp.sum(first_part * first_part),
                        jnp.sum(second_part * second_part),
                    ]
                )
                for first_part, second_part in zip(first_parts, second_parts)
            ]
        )
        totals = group_totals(partial_value, bit_pos, depth_count)
        grad_parts = weigh_pair(first_parts, second_parts, totals)
    return (grad_parts[0], grad_parts[1], grad_parts[2], grad_parts[3])


def solution(mesh):
    placed = (
        P(("node", "replica"), None),
        P(("node", "replica"), None),
        P(("node", "replica")),
        P(None, "node"),
        P("node"),
        P("node", None),
    )
    return jax.shard_map(
        body,
        mesh=mesh,
        in_specs=placed,
        out_specs=(
            P("replica", "node"),
            P(("node", "replica"), None),
            P(("node", "replica")),
            P(("node", "replica")),
        ),
        check_vma=False,
    )
```

profile of v0, /device:TPU:1, one launch (start us, length us, event | category | flops | bytes accessed | tf_op | source)
XLA Modules:
  0.0 620.3 jit_solution(7858094761799900455)
XLA Ops:
  9.4 2.8 pad_maximum_fusion.1
  12.3 89.3 %all-gather.2.cloned.1.call-done = bf16[2048,2048]{1,0:T(8,128)(2,1)} async-done(((bf16[512,2048]{1,0:T(8,128)(2,1)}), bf16[2048,2048]{1,0:T(8,128)(2,1)}) %all-gather.2.cloned.1.call-update) | async-done | bytes 8388624 | tf_op jit(solution)/shard_map/all_gather | solution.py:34
  101.6 3.0 convert_reduce_fusion
  104.8 4.7 fusion.6
  109.5 4.2 fusion.26
  113.8 2.5 fusion.8
  116.7 2.4 fusion.4
  121.0 5.4 collective-permute-start
  126.5 78.7 %collective-permute-done = f32[524672]{0:T(1024)} collective-permute-done((f32[524672]{0:T(1024)}, f32[524672]{0:T(1024)}, u32[]{:S(2)}, u32[]{:S(2)}) %collective-permute-start) | collective-permute-done | bytes 2098720 | tf_op jit(solution)/shard_map/ppermute | solution.py:29
  205.2 3.0 fusion.14
  210.6 4.3 multiply_reduce_fusion.5
  217.2 3.6 multiply_reduce_fusion.2
  223.5 3.9 maximum_bitcast_fusion.2
  227.3 3.9 maximum_bitcast_fusion
  231.9 5.8 all-to-all-start
  237.7 4.2 all-to-all-done
  241.9 7.0 %collective-permute-start.1 = (f32[4,3]{0,1:T(4,128)S(1)}, f32[4,3]{0,1:T(4,128)S(1)}, u32[]{:S(2)}, u32[]{:S(2)}) collective-permute-start(f32[4,3]{0,1:T(4,128)S(1)} %reduce_sum.734), channel_id=1, source_target_pairs={{0,32},{1,33},{2,34},{3,35},{4,36},{5,37},{6,38},{7,39},{8,40},{9,... | collective-permute-start | bytes 152 | tf_op jit(solution)/shard_map/ppermute | solution.py:29
  265.9 11.8 %collective-permute-start.2 = (f32[262336]{0:T(1024)}, f32[262336]{0:T(1024)}, u32[]{:S(2)}, u32[]{:S(2)}) collective-permute-start(f32[262336]{0:T(1024)} %pad_maximum_fusion.2), channel_id=1, source_target_pairs={{0,16},{1,17},{2,18},{3,19},{4,20},{5,21},{6,22},{7,23},{8,24},{9,... | collective-permute-start | bytes 3148040 | tf_op jit(solution)/shard_map/ppermute | solution.py:29
  277.6 46.1 %collective-permute-done.2 = f32[262336]{0:T(1024)} collective-permute-done((f32[262336]{0:T(1024)}, f32[262336]{0:T(1024)}, u32[]{:S(2)}, u32[]{:S(2)}) %collective-permute-start.2) | collective-permute-done | bytes 1049376 | tf_op jit(solution)/shard_map/ppermute | solution.py:29
  328.0 2.8 multiply_reduce_fusion.11
  345.3 3.2 all-to-all-start.1
  348.5 4.1 all-to-all-done.1
  352.8 3.3 collective-permute-done.3
  356.1 6.3 %collective-permute-done.4 = f32[4,3]{0,1:T(4,128)S(1)} collective-permute-done((f32[4,3]{0,1:T(4,128)S(1)}, f32[4,3]{0,1:T(4,128)S(1)}, u32[]{:S(2)}, u32[]{:S(2)}) %collective-permute-start.4) | collective-permute-done | bytes 80 | tf_op jit(solution)/shard_map/ppermute | solution.py:29
  376.3 9.7 %collective-permute-done.5 = f32[131168]{0:T(1024)} collective-permute-done((f32[131168]{0:T(1024)S(1)}, f32[131168]{0:T(1024)}, u32[]{:S(2)}, u32[]{:S(2)}) %collective-permute-start.5) | collective-permute-done | bytes 524704 | tf_op jit(solution)/shard_map/ppermute | solution.py:29
  400.1 3.2 all-to-all-start.2
  403.4 4.1 all-to-all-done.2
  410.3 3.1 collective-permute-done.7
  414.1 5.6 collective-permute-done.8
  431.1 2.7 collective-permute-start.9
  433.8 4.0 collective-permute-done.9
  449.4 3.2 all-to-all-start.3
  452.7 4.1 all-to-all-done.3
  456.8 2.8 collective-permute-start.10
  463.6 3.1 collective-permute-done.12
  467.4 5.6 collective-permute-done.13
  485.6 3.0 collective-permute-done.14
  500.0 3.2 all-to-all-start.4
  503.3 4.1 all-to-all-done.4
  509.9 2.7 collective-permute-start.16
  516.6 3.1 collective-permute-done.18
  520.4 5.7 collective-permute-done.19
  537.1 24.0 %collective-permute-start.20 = (f32[16396]{0:T(1024)S(1)}, f32[16396]{0:T(1024)S(1)}, u32[]{:S(2)}, u32[]{:S(2)}) collective-permute-start(f32[16396]{0:T(1024)S(1)} %concatenate.27), channel_id=1, source_target_pairs={{0,1},{1,0},{2,3},{3,2},{4,5},{5,4},{6,7},{7,6},{8,9},{9,8},{10,11... | collective-permute-start | bytes 196760 | tf_op jit(solution)/shard_map/ppermute | solution.py:29
  572.9 6.5 %all_to_all.30 = f32[4,4,3]{1,2,0:T(4,128)S(1)} all-to-all(f32[4,4,3]{1,2,0:T(4,128)S(1)} %broadcast_in_dim.29), channel_id=1, replica_groups=mesh['node'=4,'replica'=64] {'node'}, dimensions={0} | all-to-all | bytes 384 | tf_op jit(solution)/shard_map/all_to_all | solution.py:16
  584.2 2.7 collective-permute-start.23
  588.2 2.4 collective-permute-done.24
  590.6 3.3 collective-permute-done.25
  595.0 5.3 collective-permute-done.26
  (224 shorter events, 120.9 us)
Async XLA Ops:
  7.2 102.3 %copy-start = (bf16[512,1024]{1,0:T(8,128)(2,1)S(1)}, bf16[512,1024]{1,0:T(8,128)(2,1)}, u32[]{:S(2)}) copy-start(bf16[512,1024]{1,0:T(8,128)(2,1)} %param.11) | copy-start | bytes 3145732
  7.2 94.4 %all-gather.2.cloned.1.call-start = ((), (), s32[]{:S(2)}) async-start(), calls=%async_computation.6 | async-start | bytes 10485760 | tf_op jit(solution)/shard_map/all_gather | solution.py:34
  8.0 4.2 copy-start.2
  12.2 92.5 %copy-start.3 = (bf16[1024,512]{1,0:T(8,128)(2,1)S(1)}, bf16[1024,512]{1,0:T(8,128)(2,1)}, u32[]{:S(2)}) copy-start(bf16[1024,512]{1,0:T(8,128)(2,1)} %param.9) | copy-start | bytes 3145732
  101.6 7.9 %slice-start = ((s8[8388608]{0:T(1024)(128)(4,1)}), s8[4194304]{0:T(1024)(128)(4,1)S(1)}, s32[]{:S(2)}) async-start(s8[8388608]{0:T(1024)(128)(4,1)} %bitcast.213), calls=%async_computation.7 | async-start | bytes 8388608
  104.8 4.8 slice-start.1
  119.1 2.0 copy-start.1
  121.0 84.2 %collective-permute-start = (f32[524672]{0:T(1024)}, f32[524672]{0:T(1024)}, u32[]{:S(2)}, u32[]{:S(2)}) collective-permute-start(f32[524672]{0:T(1024)} %pad_maximum_fusion), channel_id=1, source_target_pairs={{0,32},{1,33},{2,34},{3,35},{4,36},{5,37},{6,38},{7,39},{8,40},{9,... | collective-permute-start | bytes 6296072 | tf_op jit(solution)/shard_map/ppermute | solution.py:29
  231.9 10.0 %all-to-all-start = ((f32[4,4,3]{1,2,0:T(4,128)}), f32[4,4,3]{1,2,0:T(4,128)S(1)}, u32[]{:S(2)}, u32[]{:S(2)}) async-start(f32[4,4,3]{1,2,0:T(4,128)} %broadcast_in_dim.24), calls=%async_computation | async-start | bytes 16384 | tf_op jit(solution)/shard_map/all_to_all | solution.py:16
  241.9 8.0 %collective-permute-start.1 = (f32[4,3]{0,1:T(4,128)S(1)}, f32[4,3]{0,1:T(4,128)S(1)}, u32[]{:S(2)}, u32[]{:S(2)}) collective-permute-start(f32[4,3]{0,1:T(4,128)S(1)} %reduce_sum.734), channel_id=1, source_target_pairs={{0,32},{1,33},{2,34},{3,35},{4,36},{5,37},{6,38},{7,39},{8,40},{9,... | collective-permute-start | bytes 152 | tf_op jit(solution)/shard_map/ppermute | solution.py:29
  265.9 57.9 %collective-permute-start.2 = (f32[262336]{0:T(1024)}, f32[262336]{0:T(1024)}, u32[]{:S(2)}, u32[]{:S(2)}) collective-permute-start(f32[262336]{0:T(1024)} %pad_maximum_fusion.2), channel_id=1, source_target_pairs={{0,16},{1,17},{2,18},{3,19},{4,20},{5,21},{6,22},{7,23},{8,24},{9,... | collective-permute-start | bytes 3148040 | tf_op jit(solution)/shard_map/ppermute | solution.py:29
  345.3 7.4 %all-to-all-start.1 = ((f32[4,4,3]{1,2,0:T(4,128)}), f32[4,4,3]{1,2,0:T(4,128)S(1)}, u32[]{:S(2)}, u32[]{:S(2)}) async-start(f32[4,4,3]{1,2,0:T(4,128)} %broadcast_in_dim.25), calls=%async_computation.1 | async-start | bytes 16384 | tf_op jit(solution)/shard_map/all_to_all | solution.py:16
  352.7 3.4 collective-permute-start.3
  356.1 6.3 %collective-permute-start.4 = (f32[4,3]{0,1:T(4,128)S(1)}, f32[4,3]{0,1:T(4,128)S(1)}, u32[]{:S(2)}, u32[]{:S(2)}) collective-permute-start(f32[4,3]{0,1:T(4,128)S(1)} %add.366), channel_id=1, source_target_pairs={{0,32},{1,33},{2,34},{3,35},{4,36},{5,37},{6,38},{7,39},{8,40},{9,... | collective-permute-start | bytes 152 | tf_op jit(solution)/shard_map/ppermute | solution.py:29
  376.3 9.7 %collective-permute-start.5 = (f32[131168]{0:T(1024)S(1)}, f32[131168]{0:T(1024)}, u32[]{:S(2)}, u32[]{:S(2)}) collective-permute-start(f32[131168]{0:T(1024)S(1)} %concatenate.24), channel_id=1, source_target_pairs={{0,8},{1,9},{2,10},{3,11},{4,12},{5,13},{6,14},{7,15},{8,0},{9,1},... | collective-permute-start | bytes 1574024 | tf_op jit(solution)/shard_map/ppermute | solution.py:29
  400.1 7.4 %all-to-all-start.2 = ((f32[4,4,3]{1,2,0:T(4,128)}), f32[4,4,3]{1,2,0:T(4,128)S(1)}, u32[]{:S(2)}, u32[]{:S(2)}) async-start(f32[4,4,3]{1,2,0:T(4,128)} %broadcast_in_dim.26), calls=%async_computation.2 | async-start | bytes 16384 | tf_op jit(solution)/shard_map/all_to_all | solution.py:16
  407.5 2.5 collective-permute-start.6
  410.0 3.3 collective-permute-start.7
  413.4 6.3 %collective-permute-start.8 = (f32[4,3]{0,1:T(4,128)S(1)}, f32[4,3]{0,1:T(4,128)S(1)}, u32[]{:S(2)}, u32[]{:S(2)}) collective-permute-start(f32[4,3]{0,1:T(4,128)S(1)} %add.381), channel_id=1, source_target_pairs={{0,32},{1,33},{2,34},{3,35},{4,36},{5,37},{6,38},{7,39},{8,40},{9,... | collective-permute-start | bytes 152 | tf_op jit(solution)/shard_map/ppermute | solution.py:29
  431.1 6.8 %collective-permute-start.9 = (f32[65584]{0:T(1024)S(1)}, f32[65584]{0:T(1024)S(1)}, u32[]{:S(2)}, u32[]{:S(2)}) collective-permute-start(f32[65584]{0:T(1024)S(1)} %concatenate.25), channel_id=1, source_target_pairs={{0,4},{1,5},{2,6},{3,7},{4,0},{5,1},{6,2},{7,3},{8,12},{9,13},{10,... | collective-permute-start | bytes 787016 | tf_op jit(solution)/shard_map/ppermute | solution.py:29
  449.4 7.4 %all-to-all-start.3 = ((f32[4,4,3]{1,2,0:T(4,128)}), f32[4,4,3]{1,2,0:T(4,128)S(1)}, u32[]{:S(2)}, u32[]{:S(2)}) async-start(f32[4,4,3]{1,2,0:T(4,128)} %broadcast_in_dim.27), calls=%async_computation.3 | async-start | bytes 16384 | tf_op jit(solution)/shard_map/all_to_all | solution.py:16
  456.8 4.0 collective-permute-start.10
  460.9 2.4 collective-permute-start.11
  463.3 3.3 collective-permute-start.12
  466.7 6.3 %collective-permute-start.13 = (f32[4,3]{0,1:T(4,128)S(1)}, f32[4,3]{0,1:T(4,128)S(1)}, u32[]{:S(2)}, u32[]{:S(2)}) collective-permute-start(f32[4,3]{0,1:T(4,128)S(1)} %add.397), channel_id=1, source_target_pairs={{0,32},{1,33},{2,34},{3,35},{4,36},{5,37},{6,38},{7,39},{8,40},{9,... | collective-permute-start | bytes 152 | tf_op jit(solution)/shard_map/ppermute | solution.py:29
  484.1 4.4 collective-permute-start.14
  500.0 7.4 %all-to-all-start.4 = ((f32[4,4,3]{1,2,0:T(4,128)}), f32[4,4,3]{1,2,0:T(4,128)S(1)}, u32[]{:S(2)}, u32[]{:S(2)}) async-start(f32[4,4,3]{1,2,0:T(4,128)} %broadcast_in_dim.28), calls=%async_computation.4 | async-start | bytes 16384 | tf_op jit(solution)/shard_map/all_to_all | solution.py:16
  507.4 2.5 collective-permute-start.15
  509.9 3.9 collective-permute-start.16
  513.9 2.4 collective-permute-start.17
  516.3 3.3 collective-permute-start.18
  519.7 6.3 %collective-permute-start.19 = (f32[4,3]{0,1:T(4,128)S(1)}, f32[4,3]{0,1:T(4,128)S(1)}, u32[]{:S(2)}, u32[]{:S(2)}) collective-permute-start(f32[4,3]{0,1:T(4,128)S(1)} %add.414), channel_id=1, source_target_pairs={{0,32},{1,33},{2,34},{3,35},{4,36},{5,37},{6,38},{7,39},{8,40},{9,... | collective-permute-start | bytes 152 | tf_op jit(solution)/shard_map/ppermute | solution.py:29
  537.1 25.0 %collective-permute-start.20 = (f32[16396]{0:T(1024)S(1)}, f32[16396]{0:T(1024)S(1)}, u32[]{:S(2)}, u32[]{:S(2)}) collective-permute-start(f32[16396]{0:T(1024)S(1)} %concatenate.27), channel_id=1, source_target_pairs={{0,1},{1,0},{2,3},{3,2},{4,5},{5,4},{6,7},{7,6},{8,9},{9,8},{10,11... | collective-permute-start | bytes 196760 | tf_op jit(solution)/shard_map/ppermute | solution.py:29
  579.4 2.4 collective-permute-start.21
  581.8 2.4 collective-permute-start.22
  584.2 3.9 collective-permute-start.23
  588.2 2.4 collective-permute-start.24
  590.6 3.3 collective-permute-start.25
  594.0 6.3 %collective-permute-start.26 = (f32[4,3]{0,1:T(4,128)S(1)}, f32[4,3]{0,1:T(4,128)S(1)}, u32[]{:S(2)}, u32[]{:S(2)}) collective-permute-start(f32[4,3]{0,1:T(4,128)S(1)} %add.432), channel_id=1, source_target_pairs={{0,32},{1,33},{2,34},{3,35},{4,36},{5,37},{6,38},{7,39},{8,40},{9,... | collective-permute-start | bytes 152 | tf_op jit(solution)/shard_map/ppermute | solution.py:29
Sparse Core Ops, SparseCore 0:
  12.4 89.2 all-gather.1
where the time goes:
time: 627 us; the launch traced here: 620 us
  waiting for transfers between devices  314 us (50%)
  other arithmetic  98.6 us (16%)
  starting transfers between devices  88.7 us (14%)
  between operations  75.2 us (12%)
  local copies, waits for them, and re-layouts  23.8 us (4%)
  matrix products  13.8 us (2%)
  blocking collectives  6.5 us (1%)
    ppermute x27, waiting for transfers between devices, from_partner(): return lax.ppermute(value, axis, pairs)  204 us
    all_gather x1, waiting for transfers between devices, in_one_piece(): filled, at, outs = (lax.all_gather(both, axis, axis=dim, tiled=True), 0, [])  89.3 us
    ppermute x27, starting transfers between devices, from_partner(): return lax.ppermute(value, axis, pairs)  69.8 us
    another operation x28, other arithmetic, body(): jnp.stack([jnp.stack([jnp.sum(first_part * second_part), jnp.sum(first_pa...  47.5 us
    reduce_sum x24, other arithmetic, body(): jnp.sum(first_part * second_part)  30.7 us
    all_to_all x5, waiting for transfers between devices, copy_for_each(): lax.all_to_all(jnp.broadcast_to(array[None], (peers, *array.shape)), axis...  20.7 us
    all_to_all x5, starting transfers between devices, copy_for_each(): lax.all_to_all(jnp.broadcast_to(array[None], (peers, *array.shape)), axis...  18.8 us
  transfers between devices with their start and end apart: 33, of which 33 were waited for; matrix products, arithmetic and copies ran while one was open for 0% of the time, Pallas kernels for 0%

commit v1 on v0

v1 whole, which is shorter than its diff:
```python
import jax
import jax.numpy as jnp
from jax import lax
from jax.experimental import pallas as pl
from jax.experimental.pallas import tpu as pltpu
from jax.sharding import PartitionSpec as P

SEQ = 128


root_half = 0.7071067811865476
inv_root_tau = 0.3989422804014327
eps_norm = 1e-06


def masked_cotangent(grads_out, lengths):
    row_count = grads_out.shape[0]
    position = lax.broadcasted_iota(jnp.int32, (row_count // SEQ, SEQ), 1)
    keep_mask = (position < lengths[:, None]).reshape(row_count, 1)
    return jnp.where(keep_mask, grads_out, jnp.zeros_like(grads_out))


def layer_grads(inputs, cotangent, w_in, bias_in, w_out):
    preact = jnp.dot(inputs, w_in, preferred_element_type=jnp.float32) + bias_in.astype(jnp.float32)
    normal_cdf = 0.5 * (1.0 + jax.scipy.special.erf(preact * root_half))
    activated = (preact * normal_cdf).astype(jnp.bfloat16)
    grad_act = lax.dot_general(
        cotangent, w_out, (((1,), (1,)), ((), ())), preferred_element_type=jnp.float32
    )
    grad_pre = grad_act * (normal_cdf + preact * inv_root_tau * jnp.exp(-0.5 * preact * preact))
    grad_half = grad_pre.astype(jnp.bfloat16)
    grad_in = lax.dot_general(
        inputs, grad_half, (((0,), (0,)), ((), ())), preferred_element_type=jnp.float32
    )
    grad_out = lax.dot_general(
        activated, cotangent, (((0,), (0,)), ((), ())), preferred_element_type=jnp.float32
    )
    return (grad_in, grad_out, jnp.sum(grad_pre, 0), jnp.sum(cotangent.astype(jnp.float32), 0))


def quantize(rows):
    top = jnp.max(jnp.abs(rows), axis=1, keepdims=True)
    unit = jnp.maximum(top, 1e-30) * (1.0 / 32767.0)
    codes = jnp.round(rows * (1.0 / unit)).astype(jnp.int16)
    return codes, unit


def fold_coefs(gram):
    count = gram.shape[-1]
    width = count
    row_of = lax.broadcasted_iota(jnp.int32, (count, count), 0)
    col_of = lax.broadcasted_iota(jnp.int32, (count, count), 1)
    weight_row = jnp.ones((1, count), jnp.float32)
    inner = gram
    while width > 1:
        half = width // 2
        first = row_of % width < half
        own = (row_of == col_of).astype(jnp.float32)
        own_row = jnp.sum(inner * own, axis=0, keepdims=True)
        own_col = jnp.sum(inner * own, axis=1, keepdims=True)
        cross = (row_of % half == col_of % half) & (row_of != col_of)
        cross = (cross & (row_of < width) & (col_of < width)).astype(jnp.float32)
        cross_row = jnp.sum(inner * cross, axis=0, keepdims=True)
        cross_col = jnp.sum(inner * cross, axis=1, keepdims=True)
        coef_row = 1.0 - cross_row / (2.0 * (own_row + eps_norm))
        coef_col = 1.0 - cross_col / (2.0 * (own_col + eps_norm))
        scaled = jnp.where((row_of < width) & (col_of < width), inner * coef_row * coef_col, 0.0)
        leaf = (row_of == col_of % width).astype(jnp.float32)
        weight_row = weight_row * jnp.sum(leaf * coef_col, axis=0, keepdims=True)
        folded = scaled + pltpu.roll(scaled, count - half, 0)
        folded = folded + pltpu.roll(folded, count - half, 1)
        inner = jnp.where((row_of < half) & (col_of < half), folded, 0.0)
        width = half
    return weight_row


def coef_kernel(gram_ref, coef_ref):
    rows = [fold_coefs(gram_ref[now]) for now in range(4)]
    coef_ref[...] = jnp.concatenate(rows + [jnp.zeros((4, rows[0].shape[1]), jnp.float32)], axis=0)


def body(inputs, grads_out, lengths, w_in, bias_in, w_out):
    cotangent = masked_cotangent(grads_out, lengths)
    node_count = lax.axis_size("node")
    replicas = lax.axis_size("replica")
    width_model = inputs.shape[1]
    both = lax.all_gather(jnp.concatenate((inputs, cotangent), axis=1), "node", axis=0, tiled=True)
    terms = layer_grads(both[:, :width_model], both[:, width_model:], w_in, bias_in, w_out)
    share = width_model // node_count
    bias_share = lax.dynamic_slice_in_dim(terms[3], lax.axis_index("node") * share, share)
    codes_in, unit_in = quantize(terms[0])
    codes_out, unit_out = quantize(terms[1])
    codes = jnp.concatenate((codes_in.reshape(replicas, -1), codes_out.reshape(replicas, -1)), axis=1)
    small = jnp.concatenate(
        [v.reshape(replicas, -1) for v in (unit_in, unit_out, terms[2], bias_share)], axis=1
    )
    codes = lax.all_to_all(codes, "replica", 0, 0, tiled=True)
    small = lax.all_to_all(small, "replica", 0, 0, tiled=True)
    rows_in = terms[0].shape[0] // replicas
    rows_out = terms[1].shape[0] // replicas
    rows_bias = terms[2].shape[0] // replicas
    size_in = terms[0].size // replicas
    part_in = codes[:, :size_in].astype(jnp.float32).reshape(replicas, rows_in, -1) * small[:, :rows_in, None]
    part_out = (
        codes[:, size_in:].astype(jnp.float32).reshape(replicas, rows_out, -1)
        * small[:, rows_in : rows_in + rows_out, None]
    )
    rest = small[:, rows_in + rows_out :]
    parts = [part_in.reshape(replicas, -1), part_out.reshape(replicas, -1), rest[:, :rows_bias], rest[:, rows_bias:]]
    gram = jnp.stack(
        [
            lax.dot_general(
                p, p, (((1,), (1,)), ((), ())), precision=lax.Precision.HIGHEST, preferred_element_type=jnp.float32
            )
            for p in parts
        ]
    )
    gram = lax.psum(gram, ("node", "replica"))
    coefs = pl.pallas_call(
        coef_kernel, out_shape=jax.ShapeDtypeStruct((8, replicas), jnp.float32), name="tree_coefs"
    )(gram)
    outs = [jnp.sum(p * coefs[now][:, None], axis=0) for now, p in enumerate(parts)]
    return (outs[0].reshape(rows_in, -1), outs[1].reshape(rows_out, -1), outs[2], outs[3])


def solution(mesh):
    placed = (
        P(("node", "replica"), None),
        P(("node", "replica"), None),
        P(("node", "replica")),
        P(None, "node"),
        P("node"),
        P("node", None),
    )
    return jax.shard_map(
        body,
        mesh=mesh,
        in_specs=placed,
        out_specs=(
            P("replica", "node"),
            P(("node", "replica"), None),
            P(("node", "replica")),
            P(("node", "replica")),
        ),
        check_vma=False,
    )
```

time: 627 us -> 483 us (0.77)
  other arithmetic: 98.6 us -> 17.9 us
  starting transfers between devices: 88.7 us -> 21.2 us
  between operations: 75.2 us -> 14.3 us
  waiting for transfers between devices: 314 us -> 374 us
  matrix products: 13.8 us -> 21.8 us
  blocking collectives: 6.5 us -> 0 us
    psum x0 -> x1, waiting for transfers between devices: none -> 242 us  [body(): gram = lax.psum(gram, ('node', 'replica'))]
    ppermute x27 -> x0, waiting for transfers between devices: 204 us -> none  [from_partner(): return lax.ppermute(value, axis, pairs)]
    ppermute x27 -> x0, starting transfers between devices: 69.8 us -> none  [from_partner(): return lax.ppermute(value, axis, pairs)]
    another operation x28 -> x1, other arithmetic: 47.5 us -> 0.67 us  [body(): jnp.stack([lax.dot_general(p, p, (((1,), (1,)), ((), ())), precision=lax....]
    reduce_sum x30 -> x3, other arithmetic: 30.8 us -> 4.5 us  [body(): jnp.sum(p * coefs[now][:, None], axis=0)]
    all_to_all x5 -> x2, waiting for transfers between devices: 20.7 us -> 43.6 us  [the longest x1 43.6 us: body(): codes = lax.all_to_all(codes, 'replica', 0, 0, tiled=True)]
    unnamed x24 -> x21, local copies, waits for them, and re-layouts: 0.98 us -> 21.8 us
    slice x12 -> x1, local copies, waits for them, and re-layouts: 10.5 us -> 0.07 us  [body(): small[:, rows_in:rows_in + rows_out, None]]
  transfers between devices with their start and end apart: 33 -> 4, of which waited for: 33 -> 3; matrix products, arithmetic and copies ran while one was open for 0% -> 3% of each run, Pallas kernels for 0% -> 0%
where the time goes in v1:
time: 483 us; the launch traced here: 482 us
  waiting for transfers between devices  374 us (77%)
  local copies, waits for them, and re-layouts  29 us (6%)
  matrix products  21.8 us (5%)
  starting transfers between devices  21.2 us (4%)
  other arithmetic  17.9 us (4%)
  between operations  14.3 us (3%)
    psum x1, waiting for transfers between devices, body(): gram = lax.psum(gram, ('node', 'replica'))  242 us
    all_gather x1, waiting for transfers between devices, body(): lax.all_gather(jnp.concatenate((inputs, cotangent), axis=1), 'node', axis...  88.7 us
    all_to_all x1, waiting for transfers between devices, body(): codes = lax.all_to_all(codes, 'replica', 0, 0, tiled=True)  43.6 us
    unnamed x21, local copies, waits for them, and re-layouts  21.8 us
    all_to_all x1, starting transfers between devices, body(): small = lax.all_to_all(small, 'replica', 0, 0, tiled=True)  10.9 us
    all_to_all x1, starting transfers between devices, body(): codes = lax.all_to_all(codes, 'replica', 0, 0, tiled=True)  10.3 us
  transfers between devices with their start and end apart: 4, of which 3 were waited for; matrix products, arithmetic and copies ran while one was open for 3% of the time, Pallas kernels for 0%

profile of v1, /device:TPU:1, one launch (start us, length us, event | category | flops | bytes accessed | tf_op | source)
XLA Modules:
  0.0 482.0 jit_solution(9522361547104059243)
XLA Ops:
  7.2 0.9 fusion.21
  8.1 1.4 broadcast_select_fusion
  9.5 1.6 pad_maximum_fusion
  11.1 0.6 copy-done.5
  11.7 88.7 %all-gather.2.cloned.1.call-done = bf16[2048,2048]{1,0:T(8,128)(2,1)} async-done(((bf16[512,2048]{1,0:T(8,128)(2,1)}), bf16[2048,2048]{1,0:T(8,128)(2,1)}) %all-gather.2.cloned.1.call-update) | async-done | bytes 8388624 | tf_op jit(solution)/shard_map/all_gather | solution.py:87
  100.5 4.7 fusion.6
  105.2 4.2 fusion.22
  109.4 2.4 abs_reduce_fusion.1
  111.8 0.3 round-nearest-even_convert_fusion.1
  112.1 1.0 copy.14
  113.2 1.4 reshape.97
  114.5 6.0 %abs_reduce_fusion = (f32[512]{0:T(512)S(1)}, f32[512,1024]{1,0:T(8,128)S(1)}) fusion(bf16[2048,2048]{1,0:T(8,128)(2,1)} %all-gather.2.cloned.1.call-done, f32[2048,512]{1,0:T(8,128)} %copy-done.7, f32[512]{0:T(512)S(1)} %convert_element_type.24), kind=kOutput, calls=%fused_computation.23 | convolution fusion | flops 2154823168 | bytes 10489856 | tf_op jit(solution)/shard_map/dot_general | solution.py:35
  120.5 0.4 round-nearest-even_convert_fusion
  120.9 1.4 reshape.98
  122.3 0.1 mul.173
  122.3 0.1 mul.174
  122.4 0.1 reshape.99
  122.5 2.9 convert_reduce_fusion
  125.4 0.1 dynamic_slice.3
  125.5 0.1 reshape.100
  125.6 0.7 pad_maximum_fusion.2
  126.3 10.9 %all-to-all-start.1 = ((f32[64,1,36]{2,1,0:T(1,128)}), f32[64,1,36]{2,1,0:T(1,128)S(1)}, u32[]{:S(2)}, u32[]{:S(2)}) async-start(f32[64,1,36]{2,1,0:T(1,128)} %bitcast.3), calls=%async_computation.1 | async-start | bytes 65536 | tf_op jit(solution)/shard_map/all_to_all | solution.py:98
  137.2 1.7 add_bitcast_fusion
  138.9 0.5 broadcast.61
  139.4 2.9 reduce
  142.3 4.5 reshape.103
  146.9 10.3 %all-to-all-start = ((s16[64,2,8192]{2,1,0:T(2,128)(2,1)}), s16[64,2,8192]{2,1,0:T(2,128)(2,1)S(1)}, u32[]{:S(2)}, u32[]{:S(2)}) async-start(s16[64,2,8192]{2,1,0:T(2,128)(2,1)} %reshape.103), calls=%async_computation | async-start | bytes 4194304 | tf_op jit(solution)/shard_map/all_to_all | solution.py:97
  157.2 0.1 slice.56
  157.3 0.2 mul.176
  157.5 2.5 copy.18
  160.0 0.2 mul.179
  160.3 2.5 copy.19
  162.8 0.3 convolution_bitcast_fusion
  163.0 0.3 convolution_bitcast_fusion.1
  163.3 43.6 %all-to-all-done = s16[64,2,8192]{2,1,0:T(2,128)(2,1)S(1)} async-done(((s16[64,2,8192]{2,1,0:T(2,128)(2,1)}), s16[64,2,8192]{2,1,0:T(2,128)(2,1)S(1)}, u32[]{:S(2)}, u32[]{:S(2)}) %all-to-all-start) | async-done | bytes 2097184 | tf_op jit(solution)/shard_map/all_to_all | solution.py:97
  206.9 6.9 %reshape.104 = s16[64,1,16384]{2,1,0:T(2,128)(2,1)} reshape(s16[64,2,8192]{2,1,0:T(2,128)(2,1)S(1)} %all-to-all-done) | data formatting | bytes 4194304
  213.8 4.6 copy.21
  218.4 2.0 fusion.16
  220.4 2.0 fusion.15
  222.4 0.7 pad_maximum_fusion.1
  223.1 242.1 %all-reduce.2.cloned.1.call-done.gram_ref = f32[4,64,64]{2,1,0:T(8,128)} async-done(((f32[4,64,64]{2,1,0:T(8,128)}), f32[4,64,64]{2,1,0:T(8,128)}) %all-reduce.2.cloned.1.call-update) | async-done | bytes 65552 | tf_op jit(solution)/shard_map/psum | solution.py:118
  465.2 3.3 tree_coefs.1
  468.5 0.8 slice_bitcast_fusion
  469.4 0.6 multiply_reduce_fusion.2
  470.0 0.6 multiply_reduce_fusion.3
  470.6 3.3 multiply_reduce_fusion
  473.9 0.6 reshape.101
  474.5 0.6 reshape.102
  (23 shorter events, 0.2 us)
Async XLA Ops:
  7.2 98.0 %copy-start = (bf16[512,1024]{1,0:T(8,128)(2,1)S(1)}, bf16[512,1024]{1,0:T(8,128)(2,1)}, u32[]{:S(2)}) copy-start(bf16[512,1024]{1,0:T(8,128)(2,1)} %param.11) | copy-start | bytes 3145732
  7.2 2.3 copy-start.4
  7.2 93.3 %all-gather.2.cloned.1.call-start = ((), (), s32[]{:S(2)}) async-start(), calls=%async_computation.2 | async-start | bytes 10485760 | tf_op jit(solution)/shard_map/all_gather | solution.py:87
  11.1 0.7 copy-start.5
  11.1 89.4 %copy-start.6 = (bf16[1024,512]{1,0:T(8,128)(2,1)S(1)}, bf16[1024,512]{1,0:T(8,128)(2,1)}, u32[]{:S(2)}) copy-start(bf16[1024,512]{1,0:T(8,128)(2,1)} %param.9) | copy-start | bytes 3145732
  100.5 4.7 copy-start.3
  105.2 4.2 copy-start.7
  126.3 20.6 %all-to-all-start.1 = ((f32[64,1,36]{2,1,0:T(1,128)}), f32[64,1,36]{2,1,0:T(1,128)S(1)}, u32[]{:S(2)}, u32[]{:S(2)}) async-start(f32[64,1,36]{2,1,0:T(1,128)} %bitcast.3), calls=%async_computation.1 | async-start | bytes 65536 | tf_op jit(solution)/shard_map/all_to_all | solution.py:98
  146.9 60.0 %all-to-all-start = ((s16[64,2,8192]{2,1,0:T(2,128)(2,1)}), s16[64,2,8192]{2,1,0:T(2,128)(2,1)S(1)}, u32[]{:S(2)}, u32[]{:S(2)}) async-start(s16[64,2,8192]{2,1,0:T(2,128)(2,1)} %reshape.103), calls=%async_computation | async-start | bytes 4194304 | tf_op jit(solution)/shard_map/all_to_all | solution.py:97
  157.2 308.1 %all-reduce.2.cloned.1.call-start = ((), (), s32[]{:S(2)}) async-start(), calls=%async_computation.3 | async-start | bytes 262144 | tf_op jit(solution)/shard_map/psum | solution.py:118
  213.8 4.6 copy-start.1
  218.4 2.0 copy-start.2
Sparse Core Ops, SparseCore 0:
  11.2 89.2 all-gather.1
  223.3 241.9 all-reduce.1

commit v2 on v1

v2 whole, which is shorter than its diff:
```python
import functools

import jax
import jax.numpy as jnp
from jax import lax
from jax.experimental import pallas as pl
from jax.experimental.pallas import tpu as pltpu
from jax.sharding import PartitionSpec as P

SEQ = 128
MESH = pl.DeviceIdType.MESH
HALF = 256

root_half = 0.7071067811865476
inv_root_tau = 0.3989422804014327
eps_norm = 1e-06


def remote(src, dst, send_sem, recv_sem, device_id):
    return pltpu.make_async_remote_copy(
        src_ref=src, dst_ref=dst, send_sem=send_sem, recv_sem=recv_sem, device_id=device_id, device_id_type=MESH
    )


def grads_kernel(
    x_ref, g_ref, len_ref, w_in, bias_ref, w_out,
    code_in, code_out, small_ref,
    xb, cb, gin, gout, bsum, csum, small, send_sem, recv_sem, own_sem,
):
    me = lax.axis_index("node")
    count = lax.axis_size("node")
    right, left = {"node": (me + 1) % count}, {"node": (me + count - 1) % count}
    barrier = pltpu.get_barrier_semaphore()
    for neighbour in (left, right):
        pl.semaphore_signal(barrier, inc=1, device_id=neighbour, device_id_type=MESH)

    own = [pltpu.make_async_copy(x_ref.at[pl.ds(h * HALF, HALF)], xb.at[h], own_sem.at[h]) for h in range(2)]
    for copy in own:
        copy.start()
    for seq in range(g_ref.shape[0] // SEQ):
        rows = lax.broadcasted_iota(jnp.int32, (SEQ, g_ref.shape[1]), 0)
        part = g_ref[seq * SEQ : (seq + 1) * SEQ, :]
        at = seq * SEQ % HALF
        cb[seq * SEQ // HALF, at : at + SEQ, :] = jnp.where(rows < len_ref[seq], part, jnp.zeros_like(part))
    gin[...] = jnp.zeros_like(gin)
    gout[...] = jnp.zeros_like(gout)
    bsum[...] = jnp.zeros_like(bsum)
    csum[...] = jnp.zeros_like(csum)
    for copy in own:
        copy.wait()
    pl.semaphore_wait(barrier, 2)

    def pair(index, src, dst, target):
        return [remote(buf.at[src], buf.at[dst], send_sem.at[t, index], recv_sem.at[t, index], target)
                for t, buf in enumerate((xb, cb))]

    to_right = [pair(0, 0, 2, right), pair(1, 1, 3, right), pair(2, 2, 6, right)]
    to_left = [pair(3, 1, 5, left), pair(4, 0, 4, left), pair(5, 5, 7, left)]

    def start(copies):
        for copy in copies:
            copy.start()

    def arrived(copies):
        for copy in copies:
            copy.wait_recv()

    def compute(first, step):
        def one(now, carry):
            at = first + step * now
            x, c = xb[at], cb[at]
            preact = jnp.dot(x, w_in[...], preferred_element_type=jnp.float32) + bias_ref[...]
            normal_cdf = 0.5 * (1.0 + lax.erf(preact * root_half))
            activated = (preact * normal_cdf).astype(jnp.bfloat16)
            grad_act = lax.dot_general(c, w_out[...], (((1,), (1,)), ((), ())), preferred_element_type=jnp.float32)
            grad_pre = grad_act * (normal_cdf + preact * inv_root_tau * jnp.exp(-0.5 * preact * preact))
            grad_half = grad_pre.astype(jnp.bfloat16)
            gin[...] += lax.dot_general(x, grad_half, (((0,), (0,)), ((), ())), preferred_element_type=jnp.float32)
            gout[...] += lax.dot_general(activated, c, (((0,), (0,)), ((), ())), preferred_element_type=jnp.float32)
            bsum[...] += jnp.sum(grad_pre, axis=0, keepdims=True)
            csum[...] += jnp.sum(c.astype(jnp.float32), axis=0, keepdims=True)
            return carry

        lax.fori_loop(0, 2, one, 0)

    for a, b in zip(to_right[:2], to_left[:2]):
        start(a)
        start(b)
    compute(0, 1)
    arrived(to_right[0])
    start(to_right[2])
    arrived(to_left[0])
    start(to_left[2])
    compute(2, 3)
    arrived(to_right[1])
    arrived(to_left[1])
    compute(3, 1)
    arrived(to_right[2])
    arrived(to_left[2])
    compute(6, 1)
    for copies in to_right + to_left:
        for copy in copies:
            copy.wait_send()

    replicas = code_in.shape[0]
    group = 8
    rows_in, rows_out, rows_bias = code_in.shape[1], code_out.shape[1], bsum.shape[1] // replicas

    def codes(values, rows, first_lane):
        top = jnp.max(jnp.abs(values), axis=1, keepdims=True)
        unit = jnp.maximum(top, 1e-30) * (1.0 / 32767.0)
        code = jnp.round(values * (1.0 / unit)).astype(jnp.int16)
        lane = lax.broadcasted_iota(jnp.int32, (group * rows, 128), 1)
        row = lax.broadcasted_iota(jnp.int32, (group * rows, 128), 0)
        placed = jnp.where(lane - first_lane == row % rows, unit, 0.0)
        return code.reshape(group, rows, values.shape[1]), jnp.sum(placed.reshape(group, rows, 128), axis=1)

    def quantize(now, carry):
        block = pl.ds(pl.multiple_of(now * group, group), group)
        values = gin[pl.ds(pl.multiple_of(now * group * rows_in, group * rows_in), group * rows_in), :]
        code_in[block], unit_in = codes(values, rows_in, 0)
        values = gout[pl.ds(pl.multiple_of(now * group * rows_out, group * rows_out), group * rows_out), :]
        code_out[block], unit_out = codes(values, rows_out, rows_in)
        small[block, :] = unit_in + unit_out
        return carry

    lax.fori_loop(0, replicas // group, quantize, 0)

    def spread(values, per, first_lane):
        width = values.shape[1]
        row = lax.broadcasted_iota(jnp.int32, (replicas, width), 0)
        lane = lax.broadcasted_iota(jnp.int32, (replicas, width), 1)
        mine = jnp.where(lane // per == row, values, 0.0)
        source = lax.broadcasted_iota(jnp.int32, (width, 128), 0)
        target = lax.broadcasted_iota(jnp.int32, (width, 128), 1)
        pick = (target - first_lane == source % per).astype(jnp.float32)
        return jnp.dot(mine, pick, precision=lax.Precision.HIGHEST, preferred_element_type=jnp.float32)

    share = csum.shape[1] // 4
    mine = csum[:, pl.ds(pl.multiple_of(me * share, share), share)]
    total = small[...] + spread(bsum[...], rows_bias, rows_in + rows_out)
    total = total + spread(mine, share // replicas, rows_in + rows_out + rows_bias)
    small_ref[...] = total.reshape(replicas, 1, 128)


def gather_and_grads(inputs, grads_out, lengths, w_in, bias_in, w_out, replicas):
    rows, width = inputs.shape
    hidden = w_in.shape[1]
    vmem = pl.BlockSpec(memory_space=pltpu.VMEM)
    return pl.pallas_call(
        grads_kernel,
        out_shape=(
            jax.ShapeDtypeStruct((replicas, width // replicas, hidden), jnp.int16),
            jax.ShapeDtypeStruct((replicas, hidden // replicas, width), jnp.int16),
            jax.ShapeDtypeStruct((replicas, 1, 128), jnp.float32),
        ),
        in_specs=[pl.BlockSpec(memory_space=pl.ANY), vmem, pl.BlockSpec(memory_space=pltpu.SMEM), vmem, vmem, vmem],
        out_specs=(vmem, vmem, vmem),
        scratch_shapes=[
            pltpu.VMEM((8, HALF, width), jnp.bfloat16),
            pltpu.VMEM((8, HALF, width), jnp.bfloat16),
            pltpu.VMEM((width, hidden), jnp.float32),
            pltpu.VMEM((hidden, width), jnp.float32),
            pltpu.VMEM((1, hidden), jnp.float32),
            pltpu.VMEM((1, width), jnp.float32),
            pltpu.VMEM((replicas, 128), jnp.float32),
            pltpu.SemaphoreType.DMA((2, 6)),
            pltpu.SemaphoreType.DMA((2, 6)),
            pltpu.SemaphoreType.DMA((2,)),
        ],
        compiler_params=pltpu.CompilerParams(collective_id=0, has_side_effects=True),
        name="gather_grads",
    )(inputs, grads_out, lengths, w_in, bias_in, w_out)


def exchange_kernel(*refs):
    srcs, dsts = refs[:3], refs[3:6]
    send_sem, recv_sem, own_sem = refs[6:]
    me = lax.axis_index("replica")
    replicas = lax.axis_size("replica")
    core, y, z = me % 2, me // 2 % 4, me // 8
    barrier = pltpu.get_barrier_semaphore()

    def greet(step, carry):
        pl.semaphore_signal(barrier, inc=1, device_id={"replica": (me + step) % replicas}, device_id_type=MESH)
        return carry

    lax.fori_loop(1, replicas, greet, 0)
    own = [pltpu.make_async_copy(s.at[me], d.at[me], own_sem.at[t]) for t, (s, d) in enumerate(zip(srcs, dsts))]
    for copy in own:
        copy.start()
    pl.semaphore_wait(barrier, replicas - 1)

    def send(step, carry):
        place = step // 2
        other_z = (z + 3 * place) % 8
        other_y = (y + place + place // 8) % 4
        other = other_z * 8 + other_y * 2 + (core + step) % 2
        for t, (s, d) in enumerate(zip(srcs, dsts)):
            remote(s.at[other], d.at[me], send_sem.at[t], recv_sem.at[t], {"replica": other}).start()
        return carry

    lax.fori_loop(1, replicas, send, 0)
    for copy in own:
        copy.wait()
    for t, (s, d) in enumerate(zip(srcs, dsts)):
        others = pl.ds(0, replicas - 1)
        all_copies = remote(s.at[others], d.at[others], send_sem.at[t], recv_sem.at[t], {"replica": (me + 1) % replicas})
        all_copies.wait_send()
        all_copies.wait_recv()


def exchange(arrays):
    anywhere = pl.BlockSpec(memory_space=pl.ANY)
    return pl.pallas_call(
        exchange_kernel,
        out_shape=tuple(jax.ShapeDtypeStruct(a.shape, a.dtype) for a in arrays),
        in_specs=[anywhere] * 3,
        out_specs=(anywhere,) * 3,
        scratch_shapes=[
            pltpu.SemaphoreType.DMA((3,)),
            pltpu.SemaphoreType.DMA((3,)),
            pltpu.SemaphoreType.DMA((3,)),
        ],
        compiler_params=pltpu.CompilerParams(collective_id=1, has_side_effects=True),
        name="exchange",
    )(*arrays)


def fold_coefs(gram):
    count = gram.shape[-1]
    width = count
    row_of = lax.broadcasted_iota(jnp.int32, (count, count), 0)
    col_of = lax.broadcasted_iota(jnp.int32, (count, count), 1)
    weight = jnp.ones((count, 1), jnp.float32)
    inner = gram
    while width > 1:
        half = width // 2
        own = (row_of == col_of).astype(jnp.float32)
        own_row = jnp.sum(inner * own, axis=0, keepdims=True)
        own_col = jnp.sum(inner * own, axis=1, keepdims=True)
        cross = (row_of % half == col_of % half) & (row_of != col_of)
        cross = (cross & (row_of < width) & (col_of < width)).astype(jnp.float32)
        cross_row = jnp.sum(inner * cross, axis=0, keepdims=True)
        cross_col = jnp.sum(inner * cross, axis=1, keepdims=True)
        coef_row = 1.0 - cross_row / (2.0 * (own_row + eps_norm))
        coef_col = 1.0 - cross_col / (2.0 * (own_col + eps_norm))
        scaled = jnp.where((row_of < width) & (col_of < width), inner * coef_row * coef_col, 0.0)
        leaf = (row_of % width == col_of).astype(jnp.float32)
        weight = weight * jnp.sum(leaf * coef_row, axis=1, keepdims=True)
        folded = scaled + pltpu.roll(scaled, count - half, 0)
        folded = folded + pltpu.roll(folded, count - half, 1)
        inner = jnp.where((row_of < half) & (col_of < half), folded, 0.0)
        width = half
    return weight


def combine_kernel(
    code_in, code_out, small_ref,
    out_in, out_out, out_small,
    raw_in, raw_out, part_in, part_out, gram, core_slot, y_slot, x_slot, z_slot, last_slot, held, send_sem, recv_sem,
):
    replicas, rows_in, hidden = code_in.shape
    rows_out, width = code_out.shape[1:]
    me, node = lax.axis_index("replica"), lax.axis_index("node")
    core, y, z = me % 2, me // 2 % 4, me // 8
    partner = {"replica": me - core + (1 - core)}
    over_y = [{"replica": z * 8 + (y + k) % 4 * 2 + core} for k in range(1, 4)]
    over_x = [{"node": (node + k) % 4} for k in range(1, 4)]
    over_z = [{"replica": (z + k) % 8 * 8 + y * 2 + core} for k in range(1, 8)]
    barrier = pltpu.get_barrier_semaphore()
    peers = [partner] + over_y + over_x + over_z
    for peer in peers:
        pl.semaphore_signal(barrier, inc=1, device_id=peer, device_id_type=MESH)

    def widen(now, carry):
        raw_in[now] = code_in[now].astype(jnp.float32)
        raw_out[now] = code_out[now].astype(jnp.float32)
        return carry

    lax.fori_loop(0, replicas, widen, 0)
    small = small_ref[...].reshape(replicas, 128)
    for row in range(rows_in):
        part_in[:, row * hidden : (row + 1) * hidden] = raw_in[:, row, :] * small[:, row : row + 1]
    for row in range(rows_out):
        part_out[:, row * width : (row + 1) * width] = raw_out[:, row, :] * small[:, rows_in + row : rows_in + row + 1]

    def products(part):
        return lax.dot_general(
            part, part, (((1,), (1,)), ((), ())), precision=lax.Precision.HIGHEST, preferred_element_type=jnp.float32
        )

    lane = lax.broadcasted_iota(jnp.int32, (replicas, 128), 1)
    first_bias = rows_in + rows_out
    rows_bias, rows_last = hidden // replicas, width // 4 // replicas
    bias_in = jnp.where((lane >= first_bias) & (lane < first_bias + rows_bias), small, 0.0)
    bias_out = jnp.where((lane >= first_bias + rows_bias) & (lane < first_bias + rows_bias + rows_last), small, 0.0)
    gram[0] = jnp.concatenate([products(part_in[...]), products(part_out[...])], axis=1)
    gram[1] = jnp.concatenate([products(bias_in), products(bias_out)], axis=1)
    pl.semaphore_wait(barrier, len(peers))

    def stage(first, source, slots, targets):
        copies = [
            remote(source, slots.at[k], send_sem.at[first + k], recv_sem.at[first + k], target)
            for k, target in enumerate(targets)
        ]
        for copy in copies:
            copy.start()
        for copy in copies:
            copy.wait()

    stage(0, gram.at[1 - core], core_slot, [partner])
    held[0] = gram[core] + core_slot[0]
    stage(1, held.at[0], y_slot, over_y)
    held[1] = held[0] + (y_slot[0] + y_slot[1] + y_slot[2])
    stage(4, held.at[1], x_slot, over_x)
    held[2] = held[1] + (x_slot[0] + x_slot[1] + x_slot[2])
    stage(7, held.at[2], z_slot, over_z)
    total = held[2]
    for k in range(7):
        total = total + z_slot[k]
    held[3] = total
    stage(14, held.at[3], last_slot, [partner])
    other = last_slot[0]
    is_first = core == 0
    main = jnp.where(is_first, total, other)
    rest = jnp.where(is_first, other, total)

    weights = [fold_coefs(g[:, s : s + replicas]) for g in (main, rest) for s in (0, replicas)]
    for row in range(rows_in):
        part = part_in[:, row * hidden : (row + 1) * hidden]
        out_in[row : row + 1, :] = jnp.sum(part * weights[0], axis=0, keepdims=True)
    for row in range(rows_out):
        part = part_out[:, row * width : (row + 1) * width]
        out_out[row : row + 1, :] = jnp.sum(part * weights[1], axis=0, keepdims=True)
    bias = bias_in * weights[2] + bias_out * weights[3]
    out_small[...] = jnp.broadcast_to(jnp.sum(bias, axis=0, keepdims=True), out_small.shape)


def combine(arrays):
    replicas, rows_in, hidden = arrays[0].shape
    rows_out, width = arrays[1].shape[1:]
    vmem = pl.BlockSpec(memory_space=pltpu.VMEM)
    return pl.pallas_call(
        combine_kernel,
        out_shape=(
            jax.ShapeDtypeStruct((rows_in, hidden), jnp.float32),
            jax.ShapeDtypeStruct((rows_out, width), jnp.float32),
            jax.ShapeDtypeStruct((8, 128), jnp.float32),
        ),
        in_specs=[vmem] * 3,
        out_specs=(vmem,) * 3,
        scratch_shapes=[
            pltpu.VMEM(arrays[0].shape, jnp.float32),
            pltpu.VMEM(arrays[1].shape, jnp.float32),
            pltpu.VMEM((replicas, rows_in * hidden), jnp.float32),
            pltpu.VMEM((replicas, rows_out * width), jnp.float32),
            pltpu.VMEM((2, replicas, 128), jnp.float32),
            pltpu.VMEM((1, replicas, 128), jnp.float32),
            pltpu.VMEM((3, replicas, 128), jnp.float32),
            pltpu.VMEM((3, replicas, 128), jnp.float32),
            pltpu.VMEM((7, replicas, 128), jnp.float32),
            pltpu.VMEM((1, replicas, 128), jnp.float32),
            pltpu.VMEM((4, replicas, 128), jnp.float32),
            pltpu.SemaphoreType.DMA((15,)),
            pltpu.SemaphoreType.DMA((15,)),
        ],
        compiler_params=pltpu.CompilerParams(collective_id=2, has_side_effects=True),
        name="combine",
    )(*arrays)


def body(inputs, grads_out, lengths, w_in, bias_in, w_out):
    replicas = lax.axis_size("replica")
    bias_row = bias_in.astype(jnp.float32).reshape(1, -1)
    arrays = gather_and_grads(inputs, grads_out, lengths, w_in, bias_row, w_out, replicas)
    arrays = exchange(arrays)
    out_in, out_out, out_small = combine(arrays)
    rows_in, rows_out = out_in.shape[0], out_out.shape[0]
    first = rows_in + rows_out
    middle = first + w_in.shape[1] // replicas
    last = middle + inputs.shape[1] // 4 // replicas
    return (out_in, out_out, out_small[0, first:middle], out_small[0, middle:last])


def solution(mesh):
    placed = (
        P(("node", "replica"), None),
        P(("node", "replica"), None),
        P(("node", "replica")),
        P(None, "node"),
        P("node"),
        P("node", None),
    )
    return jax.shard_map(
        body,
        mesh=mesh,
        in_specs=placed,
        out_specs=(
            P("replica", "node"),
            P(("node", "replica"), None),
            P(("node", "replica")),
            P(("node", "replica")),
        ),
        check_vma=False,
    )
```

time: 483 us -> 175 us (0.36)
  waiting for transfers between devices: 374 us -> 0 us
  Pallas kernels: 3.31 us -> 168 us
  local copies, waits for them, and re-layouts: 29 us -> 4.52 us
  matrix products: 21.8 us -> 0 us
  starting transfers between devices: 21.2 us -> 0 us
  other arithmetic: 17.9 us -> 1.26 us
  between operations: 14.3 us -> 0.66 us
    psum x1 -> x0, waiting for transfers between devices: 242 us -> none  [body(): gram = lax.psum(gram, ('node', 'replica'))]
    pallas_call x1 -> x3, Pallas kernels: 3.31 us -> 168 us  [the longest x1 79.4 us: gather_and_grads(): pl.pallas_call(grads_kernel, out_shape=(jax.ShapeDtypeStruct((replicas, w...]
    all_gather x1 -> x0, waiting for transfers between devices: 88.7 us -> none  [body(): lax.all_gather(jnp.concatenate((inputs, cotangent), axis=1), 'node', axis...]
    all_to_all x2 -> x0, waiting for transfers between devices: 43.6 us -> none  [the longest x1 43.6 us: body(): codes = lax.all_to_all(codes, 'replica', 0, 0, tiled=True)]
    dot_general x8 -> x0, matrix products: 21.8 us -> none  [the longest x1 5.97 us: layer_grads(): lax.dot_general(activated, cotangent, (((0,), (0,)), ((), ())), preferred...]
    all_to_all x2 -> x0, starting transfers between devices: 21.2 us -> none  [the longest x1 10.9 us: body(): small = lax.all_to_all(small, 'replica', 0, 0, tiled=True)]
    unnamed x21 -> x4, local copies, waits for them, and re-layouts: 21.8 us -> 2 us
    reduce_sum x4 -> x0, other arithmetic: 7.37 us -> none  [the longest x3 4.5 us: body(): jnp.sum(p * coefs[now][:, None], axis=0)]
  transfers between devices with their start and end apart: 4 -> 0, of which waited for: 3 -> 0; matrix products, arithmetic and copies ran while one was open for 3% -> 0% of each run, Pallas kernels for 0% -> 0%
where the time goes in v2:
time: 175 us
  Pallas kernels  168 us (96%)
  local copies, waits for them, and re-layouts  4.52 us (3%)
    pallas_call x1, Pallas kernels, gather_and_grads(): pl.pallas_call(grads_kernel, out_shape=(jax.ShapeDtypeStruct((replicas, w...  79.4 us
    pallas_call x1, Pallas kernels, exchange(): pl.pallas_call(exchange_kernel, out_shape=tuple((jax.ShapeDtypeStruct(a.s...  61.1 us
    pallas_call x1, Pallas kernels, combine(): pl.pallas_call(combine_kernel, out_shape=(jax.ShapeDtypeStruct((rows_in,...  27.9 us

profile of v2, /device:TPU:1, one launch (start us, length us, event | category | flops | bytes accessed | tf_op | source)
XLA Modules:
  0.0 174.7 jit_solution(17955193779198008318)
XLA Ops:
  0.6 1.3 reshape.15
  1.9 79.4 %gather_grads.1 = (s16[64,16,512]{2,1,0:T(8,128)(2,1)}, s16[64,8,1024]{2,1,0:T(8,128)(2,1)}, f32[64,1,128]{2,1,0:T(1,128)}) custom-call(bf16[512,1024]{1,0:T(8,128)(2,1)} %x_ref.1, bf16[512,1024]{1,0:T(8,128)(2,1)} %g_ref.1, s32[4]{0:T(128)} %len_ref.1, bf16[1024,512]{1,0:T(8,128)(2,1)} %w_in.1, f32[1,512]{1,0:T(1,128)} %bitcast.5, bf16[512,1024]{1,0:T(8,128)(2,1)} %w_out.1), custom_call_target="tpu_custom_call" | custom-call | tf_op jit(solution)/shard_map/gather_grads/pallas_call | solution.py:150
  81.3 61.1 %exchange.1 = (s16[64,16,512]{2,1,0:T(8,128)(2,1)}, s16[64,8,1024]{2,1,0:T(8,128)(2,1)}, f32[64,1,128]{2,1,0:T(1,128)}) custom-call(s16[64,16,512]{2,1,0:T(8,128)(2,1)} %get-tuple-element.13.refs_0_, s16[64,8,1024]{2,1,0:T(8,128)(2,1)} %get-tuple-element.14.refs_1_, f32[64,1,128]{2,1,0:T(1,128)} %get-tuple-element.15.refs_2_), custom_call_target="tpu_custom_call" | custom-call | tf_op jit(solution)/shard_map/exchange/pallas_call | solution.py:215
  142.3 27.9 %combine.1 = (f32[16,512]{1,0:T(8,128)}, f32[8,1024]{1,0:T(8,128)}, f32[8,128]{1,0:T(8,128)}) custom-call(s16[64,16,512]{2,1,0:T(8,128)(2,1)} %get-tuple-element.16.code_in, s16[64,8,1024]{2,1,0:T(8,128)(2,1)} %get-tuple-element.17.code_out, f32[64,1,128]{2,1,0:T(1,128)} %get-tuple-element.18.small_ref), custom_call_target="tpu_custom_call" | custom-call | tf_op jit(solution)/shard_map/combine/pallas_call | solution.py:344
  170.2 1.3 slice_bitcast_fusion
  171.5 1.3 slice_bitcast_fusion.1
  172.7 0.0 copy-start
  172.7 1.4 copy.12
  174.1 0.0 copy-done
  174.1 0.6 copy.13
Async XLA Ops:
  172.7 1.4 copy-start

commit v3 on v2

v3 whole, which is shorter than its diff:
```python
import jax
import jax.numpy as jnp
from jax import lax
from jax.experimental import pallas as pl
from jax.experimental.pallas import tpu as pltpu
from jax.sharding import PartitionSpec as P

SEQ = 128
MESH = pl.DeviceIdType.MESH
HALF = 256

root_half = 0.7071067811865476
inv_root_tau = 0.3989422804014327
eps_norm = 1e-06


def remote(src, dst, send_sem, recv_sem, device_id):
    return pltpu.make_async_remote_copy(
        src_ref=src, dst_ref=dst, send_sem=send_sem, recv_sem=recv_sem, device_id=device_id, device_id_type=MESH
    )


def grads_kernel(
    x_ref, g_ref, len_ref, w_in, bias_ref, w_out,
    all_in, all_out, all_small,
    xb, cb, gb, wi, wo, gin, gout, bsum, csum, small, code_in, code_out, small_msg,
    load_sem, send_sem, recv_sem, relay_send, relay_recv, out_send, in_recv, rows_recv, small_recv, own_sem,
):
    node, nodes = lax.axis_index("node"), lax.axis_size("node")
    me, replicas = lax.axis_index("replica"), lax.axis_size("replica")
    core, y, z = me % 2, me // 2 % 4, me // 8
    hidden = wi.shape[1]
    right, left = {"node": (node + 1) % nodes}, {"node": (node + nodes - 1) % nodes}
    partner = {"replica": me - core + (1 - core)}
    barrier = pltpu.get_barrier_semaphore()
    for neighbour in (left, right):
        pl.semaphore_signal(barrier, inc=1, device_id=neighbour, device_id_type=MESH)

    def greet(step, carry):
        pl.semaphore_signal(barrier, inc=1, device_id={"replica": (me + step) % replicas}, device_id_type=MESH)
        return carry

    lax.fori_loop(1, replicas, greet, 0)

    columns = pl.ds(pl.multiple_of(core * hidden, hidden), hidden)
    loads = [
        pltpu.make_async_copy(g_ref, gb, load_sem.at[0]),
        pltpu.make_async_copy(x_ref.at[pl.ds(0, HALF)], xb.at[core * 8], load_sem.at[1]),
        pltpu.make_async_copy(x_ref.at[pl.ds(HALF, HALF)], xb.at[core * 8 + 1], load_sem.at[2]),
        pltpu.make_async_copy(w_in.at[:, columns], wi, load_sem.at[3]),
        pltpu.make_async_copy(w_out.at[columns], wo, load_sem.at[4]),
    ]
    for copy in loads:
        copy.start()
    loads[0].wait()
    for seq in range(g_ref.shape[0] // SEQ):
        rows = lax.broadcasted_iota(jnp.int32, (SEQ, g_ref.shape[1]), 0)
        part = gb[seq * SEQ : (seq + 1) * SEQ, :]
        at = seq * SEQ % HALF
        cb[core * 8 + seq * SEQ // HALF, at : at + SEQ, :] = jnp.where(rows < len_ref[seq], part, jnp.zeros_like(part))
    for copy in loads[1:]:
        copy.wait()
    pl.semaphore_wait(barrier, replicas + 1)

    def pair(index, src, dst, target):
        return [remote(buf.at[core * 8 + src], buf.at[core * 8 + dst], send_sem.at[t, index], recv_sem.at[t, index], target)
                for t, buf in enumerate((xb, cb))]

    to_right = [pair(0, 0, 2, right), pair(1, 1, 3, right), pair(2, 2, 6, right)]
    to_left = [pair(3, 1, 5, left), pair(4, 0, 4, left), pair(5, 5, 7, left)]

    def relay(owner, chunk):
        return [remote(buf.at[owner * 8 + chunk], buf.at[owner * 8 + chunk], relay_send.at[t, chunk],
                       relay_recv.at[t, chunk], partner) for t, buf in enumerate((xb, cb))]

    def start(copies):
        for copy in copies:
            copy.start()

    def arrived(copies):
        for copy in copies:
            copy.wait_recv()

    def left_here(copies):
        for copy in copies:
            copy.wait_send()

    def send_own():
        for a, b in zip(to_right[:2], to_left[:2]):
            start(a)
            start(b)

    @pl.when(core == 0)
    def _():
        send_own()

    start(relay(core, 0))
    start(relay(core, 1))

    rows_in, rows_out = code_in.shape[2], code_out.shape[2]
    rows_bias = rows_out
    group = 8
    bias = bias_ref[:, columns]

    def codes(values, count, rows, first_lane):
        top = jnp.max(jnp.abs(values), axis=1, keepdims=True)
        unit = jnp.maximum(top, 1e-30) * (1.0 / 32767.0)
        code = jnp.round(values * (1.0 / unit)).astype(jnp.int16)
        lane = lax.broadcasted_iota(jnp.int32, (count * rows, 128), 1)
        row = lax.broadcasted_iota(jnp.int32, (count * rows, 128), 0)
        placed = jnp.where(lane - first_lane == row % rows, unit, 0.0)
        return code.reshape(count, rows, values.shape[1]), jnp.sum(placed.reshape(count, rows, 128), axis=1)

    def spread(values, targets, per, first_lane):
        width = values.shape[1]
        row = lax.broadcasted_iota(jnp.int32, (targets, width), 0)
        lane = lax.broadcasted_iota(jnp.int32, (targets, width), 1)
        mine = jnp.where(lane // per == row, values, 0.0)
        source = lax.broadcasted_iota(jnp.int32, (width, 128), 0)
        target = lax.broadcasted_iota(jnp.int32, (width, 128), 1)
        pick = (target - first_lane == source % per).astype(jnp.float32)
        return jnp.dot(mine, pick, precision=lax.Precision.HIGHEST, preferred_element_type=jnp.float32)

    def one_replica(owner, carry):
        mine = core == owner

        def compute(chunks):
            first, step, count = chunks

            def one(now, carry):
                at = owner * 8 + first + step * now
                x, c = xb[at], cb[at]
                preact = jnp.dot(x, wi[...], preferred_element_type=jnp.float32) + bias
                normal_cdf = 0.5 * (1.0 + lax.erf(preact * root_half))
                activated = (preact * normal_cdf).astype(jnp.bfloat16)
                grad_act = lax.dot_general(c, wo[...], (((1,), (1,)), ((), ())), preferred_element_type=jnp.float32)
                grad_pre = grad_act * (normal_cdf + preact * inv_root_tau * jnp.exp(-0.5 * preact * preact))
                grad_half = grad_pre.astype(jnp.bfloat16)
                gout[...] += lax.dot_general(activated, c, (((0,), (0,)), ((), ())), preferred_element_type=jnp.float32)
                gin[...] += lax.dot_general(grad_half, x, (((0,), (0,)), ((), ())), preferred_element_type=jnp.float32)
                bsum[...] += jnp.sum(grad_pre, axis=0, keepdims=True)
                csum[...] += jnp.sum(c.astype(jnp.float32), axis=0, keepdims=True)
                return carry

            lax.fori_loop(0, count, one, 0)

        def receive(ring, chunks, forwards=()):
            @pl.when(mine)
            def _():
                for copies, chunk in zip(ring, chunks):
                    arrived(copies)
                for copies in forwards:
                    start(copies)
                for chunk in chunks:
                    start(relay(owner, chunk))

            @pl.when(jnp.logical_not(mine))
            def _():
                for chunk in chunks:
                    arrived(relay(owner, chunk))

        gin[...] = jnp.zeros_like(gin)
        gout[...] = jnp.zeros_like(gout)
        bsum[...] = jnp.zeros_like(bsum)
        csum[...] = jnp.zeros_like(csum)

        @pl.when(jnp.logical_not(mine))
        def _():
            arrived(relay(owner, 0))
            arrived(relay(owner, 1))

        receive((to_right[0], to_left[0]), (2, 5), (to_right[2], to_left[2]))
        compute((0, 1, 2))
        compute((2, 3, 2))
        receive((to_right[1], to_left[1]), (3, 4))

        @pl.when(jnp.logical_and(owner == 0, core == 1))
        def _():
            send_own()

        compute((3, 1, 2))
        receive((to_right[2], to_left[2]), (6, 7))
        compute((6, 1, 2))

        def quantize(now, carry):
            width = group * rows_in
            values = gin[:, pl.ds(pl.multiple_of(now * width, width), width)].T
            block = pl.ds(pl.multiple_of(now * group, group), group)
            code_in[owner, block], small[block, :] = codes(values, group, rows_in, 0)
            return carry

        lax.fori_loop(0, replicas // group, quantize, 0)
        half = replicas // 2

        def quantize_out(now, carry):
            height = group * rows_out
            values = gout[pl.ds(pl.multiple_of(now * height, height), height), :]
            code_out[owner, pl.ds(pl.multiple_of(now * group, group), group)], unit = codes(values, group, rows_out, rows_in)
            at = pl.multiple_of(core * half + now * group, group)
            small[pl.ds(at, group), :] += unit
            return carry

        lax.fori_loop(0, half // group, quantize_out, 0)
        kept = pl.ds(pl.multiple_of(core * half, half), half)
        small[kept, :] += spread(bsum[...], half, rows_bias, rows_in + rows_out)
        share = csum.shape[1] // 4
        mine_now = csum[:, pl.ds(pl.multiple_of(node * share, share), share)]
        total = small[...] + spread(mine_now, replicas, share // replicas, rows_in + rows_out + rows_bias)
        small_msg[owner] = total.reshape(replicas, 1, 128)

        source = me - core + owner
        pltpu.make_async_copy(code_in.at[owner, me], all_in.at[core, source], own_sem.at[owner, 0]).start()
        pltpu.make_async_copy(small_msg.at[owner, me], all_small.at[core, source], own_sem.at[owner, 1]).start()

        @pl.when(me // half == core)
        def _():
            pltpu.make_async_copy(code_out.at[owner, me % half], all_out.at[source], own_sem.at[owner, 2]).start()

        def send(step, carry):
            place = step // 2
            other_z = (z + 3 * place) % 8
            other_y = (y + place + place // 8) % 4
            other = other_z * 8 + other_y * 2 + (core + step) % 2
            target = {"replica": other}
            remote(code_in.at[owner, other], all_in.at[core, source], out_send.at[owner, 0], in_recv.at[core], target).start()
            remote(
                small_msg.at[owner, other], all_small.at[core, source], out_send.at[owner, 1], small_recv.at[core], target
            ).start()

            @pl.when(other // half == core)
            def _():
                remote(
                    code_out.at[owner, other % half], all_out.at[source], out_send.at[owner, 2], rows_recv, target
                ).start()

            return carry

        lax.fori_loop(1, replicas, send, 0)
        return carry

    lax.fori_loop(0, 2, one_replica, 0)

    for copies in to_right + to_left:
        left_here(copies)
    for chunk in range(8):
        left_here(relay(core, chunk))
    half = replicas // 2
    keeps = me // half == core
    others = pl.ds(0, replicas - 1)
    for owner in range(2):
        pltpu.make_async_copy(code_in.at[owner, me], all_in.at[core, me], own_sem.at[owner, 0]).wait()
        pltpu.make_async_copy(small_msg.at[owner, me], all_small.at[core, me], own_sem.at[owner, 1]).wait()
        remote(code_in.at[owner, others], all_in.at[core, others], out_send.at[owner, 0], in_recv.at[core], partner).wait_send()
        remote(
            small_msg.at[owner, others], all_small.at[core, others], out_send.at[owner, 1], small_recv.at[core], partner
        ).wait_send()

        @pl.when(keeps)
        def _():
            some = pl.ds(0, half - 1)
            pltpu.make_async_copy(code_out.at[owner, me % half], all_out.at[me], own_sem.at[owner, 2]).wait()
            remote(code_out.at[owner, some], all_out.at[some], out_send.at[owner, 2], rows_recv, partner).wait_send()

        @pl.when(jnp.logical_not(keeps))
        def _():
            every = pl.ds(0, half)
            remote(code_out.at[owner, every], all_out.at[every], out_send.at[owner, 2], rows_recv, partner).wait_send()

    most = pl.ds(0, replicas - 2)
    remote(all_in.at[core, most], all_in.at[core, most], out_send.at[0, 0], in_recv.at[core], partner).wait_recv()
    remote(all_in.at[1 - core], all_in.at[1 - core], out_send.at[0, 0], in_recv.at[1 - core], partner).wait_recv()
    remote(all_small.at[core, most], all_small.at[core, most], out_send.at[0, 1], small_recv.at[core], partner).wait_recv()
    remote(all_small.at[1 - core], all_small.at[1 - core], out_send.at[0, 1], small_recv.at[1 - core], partner).wait_recv()

    @pl.when(keeps)
    def _():
        remote(all_out.at[most], all_out.at[most], out_send.at[0, 2], rows_recv, partner).wait_recv()

    @pl.when(jnp.logical_not(keeps))
    def _():
        remote(all_out, all_out, out_send.at[0, 2], rows_recv, partner).wait_recv()


def gather_and_grads(inputs, grads_out, lengths, w_in, bias_in, w_out, replicas):
    rows, width = inputs.shape
    hidden = w_in.shape[1] // 2
    rows_in, rows_out = width // replicas, 2 * hidden // replicas
    vmem = pl.BlockSpec(memory_space=pltpu.VMEM)
    anywhere = pl.BlockSpec(memory_space=pl.ANY)
    return pl.pallas_call(
        grads_kernel,
        out_shape=(
            jax.ShapeDtypeStruct((2, replicas, rows_in, hidden), jnp.int16),
            jax.ShapeDtypeStruct((replicas, rows_out, width), jnp.int16),
            jax.ShapeDtypeStruct((2, replicas, 1, 128), jnp.float32),
        ),
        in_specs=[anywhere, anywhere, pl.BlockSpec(memory_space=pltpu.SMEM), anywhere, vmem, anywhere],
        out_specs=(anywhere, anywhere, anywhere),
        scratch_shapes=[
            pltpu.VMEM((16, HALF, width), jnp.bfloat16),
            pltpu.VMEM((16, HALF, width), jnp.bfloat16),
            pltpu.VMEM((rows, width), jnp.bfloat16),
            pltpu.VMEM((width, hidden), jnp.bfloat16),
            pltpu.VMEM((hidden, width), jnp.bfloat16),
            pltpu.VMEM((hidden, width), jnp.float32),
            pltpu.VMEM((hidden, width), jnp.float32),
            pltpu.VMEM((1, hidden), jnp.float32),
            pltpu.VMEM((1, width), jnp.float32),
            pltpu.VMEM((replicas, 128), jnp.float32),
            pltpu.VMEM((2, replicas, rows_in, hidden), jnp.int16),
            pltpu.VMEM((2, replicas // 2, rows_out, width), jnp.int16),
            pltpu.VMEM((2, replicas, 1, 128), jnp.float32),
            pltpu.SemaphoreType.DMA((5,)),
            pltpu.SemaphoreType.DMA((2, 6)),
            pltpu.SemaphoreType.DMA((2, 6)),
            pltpu.SemaphoreType.DMA((2, 8)),
            pltpu.SemaphoreType.DMA((2, 8)),
            pltpu.SemaphoreType.DMA((2, 3)),
            pltpu.SemaphoreType.DMA((2,)),
            pltpu.SemaphoreType.DMA,
            pltpu.SemaphoreType.DMA((2,)),
            pltpu.SemaphoreType.DMA((2, 3)),
        ],
        compiler_params=pltpu.CompilerParams(collective_id=0, has_side_effects=True),
        name="gather_grads",
    )(inputs, grads_out, lengths, w_in, bias_in, w_out)


def fold_coefs(gram):
    count = gram.shape[-1]
    width = count
    row_of = lax.broadcasted_iota(jnp.int32, (count, count), 0)
    col_of = lax.broadcasted_iota(jnp.int32, (count, count), 1)
    weight = jnp.ones((count, 1), jnp.float32)
    inner = gram
    while width > 1:
        half = width // 2
        own = (row_of == col_of).astype(jnp.float32)
        own_row = jnp.sum(inner * own, axis=0, keepdims=True)
        own_col = jnp.sum(inner * own, axis=1, keepdims=True)
        cross = (row_of % half == col_of % half) & (row_of != col_of)
        cross = (cross & (row_of < width) & (col_of < width)).astype(jnp.float32)
        cross_row = jnp.sum(inner * cross, axis=0, keepdims=True)
        cross_col = jnp.sum(inner * cross, axis=1, keepdims=True)
        coef_row = 1.0 - cross_row / (2.0 * (own_row + eps_norm))
        coef_col = 1.0 - cross_col / (2.0 * (own_col + eps_norm))
        scaled = jnp.where((row_of < width) & (col_of < width), inner * coef_row * coef_col, 0.0)
        leaf = (row_of % width == col_of).astype(jnp.float32)
        weight = weight * jnp.sum(leaf * coef_row, axis=1, keepdims=True)
        folded = scaled + pltpu.roll(scaled, count - half, 0)
        folded = folded + pltpu.roll(folded, count - half, 1)
        inner = jnp.where((row_of < half) & (col_of < half), folded, 0.0)
        width = half
    return weight


def combine_kernel(
    code_in, code_out, small_ref,
    out_in, out_out, out_small,
    raw_in, raw_out, part_in, part_out, gram, core_slot, y_slot, x_slot, z_slot, last_slot, held, send_sem, recv_sem,
):
    replicas, rows_in, hidden = raw_in.shape
    rows_out, width = code_out.shape[1:]
    me, node = lax.axis_index("replica"), lax.axis_index("node")
    core, y, z = me % 2, me // 2 % 4, me // 8
    partner = {"replica": me - core + (1 - core)}
    over_y = [{"replica": z * 8 + (y + k) % 4 * 2 + core} for k in range(1, 4)]
    over_x = [{"node": (node + k) % 4} for k in range(1, 4)]
    over_z = [{"replica": (z + k) % 8 * 8 + y * 2 + core} for k in range(1, 8)]
    barrier = pltpu.get_barrier_semaphore()
    peers = [partner] + over_y + over_x + over_z
    for peer in peers:
        pl.semaphore_signal(barrier, inc=1, device_id=peer, device_id_type=MESH)

    def widen(now, carry):
        raw_in[now, :, : hidden // 2] = code_in[0, now].astype(jnp.float32)
        raw_in[now, :, hidden // 2 :] = code_in[1, now].astype(jnp.float32)
        raw_out[now] = code_out[now].astype(jnp.float32)
        return carry

    lax.fori_loop(0, replicas, widen, 0)
    halves = [small_ref[half].reshape(replicas, 128) for half in range(2)]
    small = jnp.where(me >= replicas // 2, halves[1], halves[0])
    for row in range(rows_in):
        for half in range(2):
            first, last = half * hidden // 2, (half + 1) * hidden // 2
            part = raw_in[:, row, first:last] * halves[half][:, row : row + 1]
            part_in[:, row * hidden + first : row * hidden + last] = part
    for row in range(rows_out):
        part_out[:, row * width : (row + 1) * width] = raw_out[:, row, :] * small[:, rows_in + row : rows_in + row + 1]

    def products(part):
        return lax.dot_general(
            part, part, (((1,), (1,)), ((), ())), precision=lax.Precision.HIGHEST, preferred_element_type=jnp.float32
        )

    lane = lax.broadcasted_iota(jnp.int32, (replicas, 128), 1)
    first_bias = rows_in + rows_out
    rows_bias, rows_last = hidden // replicas, width // 4 // replicas
    bias_in = jnp.where((lane >= first_bias) & (lane < first_bias + rows_bias), small, 0.0)
    bias_out = jnp.where((lane >= first_bias + rows_bias) & (lane < first_bias + rows_bias + rows_last), small, 0.0)
    gram[0] = jnp.concatenate([products(part_in[...]), products(part_out[...])], axis=1)
    gram[1] = jnp.concatenate([products(bias_in), products(bias_out)], axis=1)
    pl.semaphore_wait(barrier, len(peers))

    def stage(first, source, slots, targets):
        copies = [
            remote(source, slots.at[k], send_sem.at[first + k], recv_sem.at[first + k], target)
            for k, target in enumerate(targets)
        ]
        for copy in copies:
            copy.start()
        for copy in copies:
            copy.wait()

    stage(0, gram.at[1 - core], core_slot, [partner])
    held[0] = gram[core] + core_slot[0]
    stage(1, held.at[0], y_slot, over_y)
    held[1] = held[0] + (y_slot[0] + y_slot[1] + y_slot[2])
    stage(4, held.at[1], x_slot, over_x)
    held[2] = held[1] + (x_slot[0] + x_slot[1] + x_slot[2])
    stage(7, held.at[2], z_slot, over_z)
    total = held[2]
    for k in range(7):
        total = total + z_slot[k]
    held[3] = total
    stage(14, held.at[3], last_slot, [partner])
    other = last_slot[0]
    is_first = core == 0
    main = jnp.where(is_first, total, other)
    rest = jnp.where(is_first, other, total)

    weights = [fold_coefs(g[:, s : s + replicas]) for g in (main, rest) for s in (0, replicas)]
    for row in range(rows_in):
        part = part_in[:, row * hidden : (row + 1) * hidden]
        out_in[row : row + 1, :] = jnp.sum(part * weights[0], axis=0, keepdims=True)
    for row in range(rows_out):
        part = part_out[:, row * width : (row + 1) * width]
        out_out[row : row + 1, :] = jnp.sum(part * weights[1], axis=0, keepdims=True)
    bias = bias_in * weights[2] + bias_out * weights[3]
    out_small[...] = jnp.broadcast_to(jnp.sum(bias, axis=0, keepdims=True), out_small.shape)


def combine(arrays):
    halves, replicas, rows_in, hidden = arrays[0].shape
    hidden = halves * hidden
    rows_out, width = arrays[1].shape[1:]
    vmem = pl.BlockSpec(memory_space=pltpu.VMEM)
    return pl.pallas_call(
        combine_kernel,
        out_shape=(
            jax.ShapeDtypeStruct((rows_in, hidden), jnp.float32),
            jax.ShapeDtypeStruct((rows_out, width), jnp.float32),
            jax.ShapeDtypeStruct((8, 128), jnp.float32),
        ),
        in_specs=[vmem] * 3,
        out_specs=(vmem,) * 3,
        scratch_shapes=[
            pltpu.VMEM((replicas, rows_in, hidden), jnp.float32),
            pltpu.VMEM(arrays[1].shape, jnp.float32),
            pltpu.VMEM((replicas, rows_in * hidden), jnp.float32),
            pltpu.VMEM((replicas, rows_out * width), jnp.float32),
            pltpu.VMEM((2, replicas, 128), jnp.float32),
            pltpu.VMEM((1, replicas, 128), jnp.float32),
            pltpu.VMEM((3, replicas, 128), jnp.float32),
            pltpu.VMEM((3, replicas, 128), jnp.float32),
            pltpu.VMEM((7, replicas, 128), jnp.float32),
            pltpu.VMEM((1, replicas, 128), jnp.float32),
            pltpu.VMEM((4, replicas, 128), jnp.float32),
            pltpu.SemaphoreType.DMA((15,)),
            pltpu.SemaphoreType.DMA((15,)),
        ],
        compiler_params=pltpu.CompilerParams(collective_id=2, has_side_effects=True),
        name="combine",
    )(*arrays)


def body(inputs, grads_out, lengths, w_in, bias_in, w_out):
    replicas = lax.axis_size("replica")
    bias_row = bias_in.astype(jnp.float32).reshape(1, -1)
    arrays = gather_and_grads(inputs, grads_out, lengths, w_in, bias_row, w_out, replicas)
    out_in, out_out, out_small = combine(arrays)
    rows_in, rows_out = out_in.shape[0], out_out.shape[0]
    first = rows_in + rows_out
    middle = first + w_in.shape[1] // replicas
    last = middle + inputs.shape[1] // 4 // replicas
    return (out_in, out_out, out_small[0, first:middle], out_small[0, middle:last])


def solution(mesh):
    placed = (
        P(("node", "replica"), None),
        P(("node", "replica"), None),
        P(("node", "replica")),
        P(None, "node"),
        P("node"),
        P("node", None),
    )
    return jax.shard_map(
        body,
        mesh=mesh,
        in_specs=placed,
        out_specs=(
            P("replica", "node"),
            P(("node", "replica"), None),
            P(("node", "replica")),
            P(("node", "replica")),
        ),
        check_vma=False,
    )
```

time: 175 us -> 152 us (0.87)
  Pallas kernels: 168 us -> 145 us
    pallas_call x2 -> x1, Pallas kernels: 140 us -> 115 us  [gather_and_grads(): pl.pallas_call(grads_kernel, out_shape=(jax.ShapeDtypeStruct((2, replicas...]
    pallas_call x1, Pallas kernels: 27.9 us -> 30 us  [combine(): pl.pallas_call(combine_kernel, out_shape=(jax.ShapeDtypeStruct((rows_in,...]
where the time goes in v3:
time: 152 us; the launch traced here: 151 us
  Pallas kernels  145 us (95%)
  local copies, waits for them, and re-layouts  4.51 us (3%)
    pallas_call x1, Pallas kernels, gather_and_grads(): pl.pallas_call(grads_kernel, out_shape=(jax.ShapeDtypeStruct((2, replicas...  115 us
    pallas_call x1, Pallas kernels, combine(): pl.pallas_call(combine_kernel, out_shape=(jax.ShapeDtypeStruct((rows_in,...  30 us

profile of v3, /device:TPU:1, one launch (start us, length us, event | category | flops | bytes accessed | tf_op | source)
XLA Modules:
  0.0 151.3 jit_solution(1797298110937390317)
XLA Ops:
  0.6 1.3 reshape.15
  1.9 114.9 %gather_grads.1 = (s16[2,64,16,256]{3,2,1,0:T(8,128)(2,1)}, s16[64,8,1024]{2,1,0:T(8,128)(2,1)}, f32[2,64,1,128]{3,2,1,0:T(1,128)}) custom-call(bf16[512,1024]{1,0:T(8,128)(2,1)} %x_ref.1, bf16[512,1024]{1,0:T(8,128)(2,1)} %g_ref.1, s32[4]{0:T(128)} %len_ref.1, bf16[1024,512]{1,0:T(8,128)(2,1)} %w_in.1, f32[1,512]{1,0:T(1,128)} %bitcast.5, ...), custom_call_target="tpu_custom_call" | custom-call | tf_op jit(solution)/shard_map/gather_grads/pallas_call | solution.py:290
  116.8 30.0 %combine.1 = (f32[16,512]{1,0:T(8,128)}, f32[8,1024]{1,0:T(8,128)}, f32[8,128]{1,0:T(8,128)}) custom-call(s16[2,64,16,256]{3,2,1,0:T(8,128)(2,1)} %get-tuple-element.10.code_in, s16[64,8,1024]{2,1,0:T(8,128)(2,1)} %get-tuple-element.11.code_out, f32[2,64,1,128]{3,2,1,0:T(1,128)} %get-tuple-element.12.small_ref), custom_call_target="tpu_custom_call" | custom-call | tf_op jit(solution)/shard_map/combine/pallas_call | solution.py:449
  146.8 1.3 slice_bitcast_fusion
  148.0 1.3 slice_bitcast_fusion.1
  149.3 0.0 copy-start
  149.3 1.4 copy.12
  150.7 0.0 copy-done
  150.7 0.6 copy.13
Async XLA Ops:
  149.3 1.4 copy-start
